TPU v7x, 32 devices: a whole 2x2x4 slice. The times are simulated.
32 devices in a mesh: parts: 1, tile: 16 (over z, y, core), face: 2 (over x), sub: 1.
Axes of the slice: x: 2, y: 2, z: 4, core: 2. Of those that a mesh axis runs over, the one named last changes fastest.
Arguments:
- fields: bfloat16 [96, 4, 32, 96], P('sub', 'face', 'tile', 'parts'), may hold values from -6 to 6
- upstream: bfloat16 [96, 4, 32, 96], P('sub', 'face', 'tile', 'parts'), may hold values from -6 to 6
- kernel_one: bfloat16 [3, 3, 96, 96], replicated, may hold values from -0.21875 to 0.21875
- kernel_two: bfloat16 [3, 3, 96, 96], replicated, may hold values from -0.21875 to 0.21875
Outputs:
- result: bfloat16 [96, 4, 32, 96], P('sub', 'face', 'tile', 'parts')
- fields_grad: bfloat16 [96, 4, 32, 96], P('sub', 'face', 'tile', 'parts')
- kernel_one_grad: float32 [3, 3, 96, 96], P('parts', None, None, 'sub')
- kernel_two_grad: float32 [3, 3, 96, 96], P('parts', None, None, 'sub')
All inputs are finite; a program needn't handle non-finite values.
Results may differ from a plain program's by a relative error of at most 0.0049.
Values may be sent and summed in bfloat16 or wider, within the bound.
A program may use at most 128 MiB of HBM per device.

v0:
```python
import jax
import jax.numpy as jnp
from jax import lax
from jax.sharding import PartitionSpec as P


def for_sending(x):

    def short(part):
        return part.astype(jnp.bfloat16) if part.dtype == jnp.float32 else part

    return jax.tree.map(short, x)


def extended(cells, sides, width):
    for axis, dim in sides:
        count = lax.axis_size(axis)
        head = lax.slice_in_dim(cells, 0, width, axis=dim)
        tail = lax.slice_in_dim(cells, cells.shape[dim] - width, cells.shape[dim], axis=dim)
        cells = jnp.concatenate(
            [
                lax.ppermute(tail, axis, [(i, (i + 1) % count) for i in range(count)]),
                cells,
                lax.ppermute(head, axis, [((i + 1) % count, i) for i in range(count)]),
            ],
            axis=dim,
        )
    return cells


def spread_2(block, axis, source):
    block = jnp.where(lax.axis_index(axis) == source, block, jnp.zeros_like(block))
    return lax.psum(block, axis)


def activate(values):
    return jax.nn.gelu(values, approximate=True)


def whole_channels(field):
    return jax.tree.map(
        lambda part, own: part.astype(own.dtype),
        lax.all_gather(for_sending(field), "sub", axis=0, tiled=True),
        field,
    )


def trade_edges(bundle):
    return extended(bundle, (("tile", 2), ("face", 1)), 1)


def copy_line(line_data, root):
    return jax.tree.map(lambda part: spread_2(part, "tile", root), line_data)


def collect_rows(pieces):
    return lax.all_gather(pieces, "tile", axis=3, tiled=True)


def select_table(tile_count, columns, offset, keep_all):
    width = columns + 2
    line_len = tile_count * columns
    source = lax.broadcasted_iota(jnp.int32, (tile_count * width, line_len), 0)
    target = lax.broadcasted_iota(jnp.int32, (tile_count * width, line_len), 1)
    place = source // width
    within = source % width
    hits = target == place * columns + within + offset
    if not keep_all:
        hits = jnp.logical_and(hits, within < columns)
    return jnp.where(hits, 1.0, 0.0).astype(jnp.float32)


def place_rows(flat_rows, table):
    return jnp.dot(
        flat_rows, table, precision=lax.Precision.HIGHEST, preferred_element_type=jnp.float32
    )


def sphere_pad_local(field):
    tile_count = lax.axis_size("tile")
    tile_place = lax.axis_index("tile")
    is_first = tile_place == 0
    is_last = tile_place == tile_count - 1
    channels, groups, columns, height = field.shape
    face_side = height // 3
    line_len = height + columns
    first_slot = jnp.concatenate([field[:, :, 0, :], field[:, :, :, 0]], axis=2)
    last_slot = jnp.concatenate([field[:, :, columns - 1, :], field[:, :, :, height - 1]], axis=2)
    got = trade_edges(jnp.stack([first_slot, last_slot], axis=2).astype(jnp.float32))
    prev_stack = got[:, 0:groups]
    own_cycle = got[:, 1 : groups + 1]
    next_stack = got[:, 2 : groups + 2]
    row_parts = jnp.stack(
        [prev_stack[:, :, 1, height:line_len], next_stack[:, :, 2, height:line_len]], axis=2
    )
    row_parts = jnp.pad(row_parts, ((0, 0), (0, 0), (0, 0), (0, 2)))
    gathered = collect_rows(row_parts)
    whole_rows = place_rows(gathered, select_table(tile_count, columns, 0, False))
    top_line = copy_line(next_stack[:, :, 1, 0:face_side], 0)
    bottom_line = copy_line(prev_stack[:, :, 2, 2 * face_side : height], tile_count - 1)
    edge_pad = ((0, 0), (0, 0), (1, 1))
    top_row = lax.dynamic_slice_in_dim(
        jnp.pad(top_line, edge_pad), tile_place * columns, columns + 2, 2
    )
    bottom_row = lax.dynamic_slice_in_dim(
        jnp.pad(bottom_line, edge_pad), tile_place * columns, columns + 2, 2
    )
    left_col = jnp.where(
        is_first,
        jnp.concatenate([whole_rows[:, :, 0], prev_stack[:, :, 0, 0 : 2 * face_side]], axis=2),
        own_cycle[:, :, 0, 0:height],
    )
    right_col = jnp.where(
        is_last,
        jnp.concatenate([next_stack[:, :, 3, face_side:height], whole_rows[:, :, 1]], axis=2),
        own_cycle[:, :, 3, 0:height],
    )
    middle = jnp.concatenate(
        [
            left_col.astype(jnp.bfloat16)[:, :, None],
            field,
            right_col.astype(jnp.bfloat16)[:, :, None],
        ],
        axis=2,
    )
    return jnp.concatenate(
        [
            top_row.astype(jnp.bfloat16)[..., None],
            middle,
            bottom_row.astype(jnp.bfloat16)[..., None],
        ],
        axis=3,
    )


def sphere_fold_local(gradient):
    tile_count = lax.axis_size("tile")
    tile_place = lax.axis_index("tile")
    is_first = tile_place == 0
    is_last = tile_place == tile_count - 1
    channels, groups, wide_cols, tall_rows = gradient.shape
    columns = wide_cols - 2
    height = tall_rows - 2
    face_side = height // 3
    line_len = height + columns
    interior = gradient[:, :, 1 : columns + 1, 1 : height + 1]
    grad_top = gradient[:, :, :, 0]
    grad_bottom = gradient[:, :, :, height + 1]
    grad_left = gradient[:, :, 0, 1 : height + 1]
    grad_right = gradient[:, :, columns + 1, 1 : height + 1]
    gathered = collect_rows(jnp.stack([grad_top, grad_bottom], axis=2))
    line_grads = place_rows(gathered, select_table(tile_count, columns, -1, True))
    prev_line = copy_line(grad_left[:, :, 0:face_side], 0)
    next_line = copy_line(grad_right[:, :, 2 * face_side : height], tile_count - 1)
    prev_piece = lax.dynamic_slice_in_dim(prev_line, tile_place * columns, columns, 2)
    next_piece = lax.dynamic_slice_in_dim(next_line, tile_place * columns, columns, 2)
    cycle = jnp.zeros((channels, groups + 2, 4, line_len), jnp.float32)
    cycle = cycle.at[:, 1 : groups + 1, 0, 0:height].add(jnp.where(is_first, 0.0, grad_left))
    cycle = cycle.at[:, 1 : groups + 1, 3, 0:height].add(jnp.where(is_last, 0.0, grad_right))
    cycle = cycle.at[:, 0:groups, 0, 0 : 2 * face_side].add(
        jnp.where(is_first, grad_left[:, :, face_side:height], 0.0)
    )
    cycle = cycle.at[:, 2 : groups + 2, 3, face_side:height].add(
        jnp.where(is_last, grad_right[:, :, 0 : 2 * face_side], 0.0)
    )
    cycle = cycle.at[:, 0:groups, 1, height:line_len].add(prev_piece)
    cycle = cycle.at[:, 2 : groups + 2, 2, height:line_len].add(next_piece)
    cycle = cycle.at[:, 2 : groups + 2, 1, 0:face_side].add(
        jnp.where(is_first, line_grads[:, :, 0], 0.0)
    )
    cycle = cycle.at[:, 0:groups, 2, 2 * face_side : height].add(
        jnp.where(is_last, line_grads[:, :, 1], 0.0)
    )
    returned = trade_edges(cycle)
    slot_sums = returned[:, :, 2:4] + jnp.concatenate(
        [returned[:, :, 0:1], returned[:, :, 5:6]], axis=2
    )
    edge_grads = (
        slot_sums[:, 2 : groups + 2]
        + jnp.pad(slot_sums[:, 0:1], ((0, 0), (0, groups - 1), (0, 0), (0, 0)))
        + jnp.pad(slot_sums[:, groups + 3 : groups + 4], ((0, 0), (groups - 1, 0), (0, 0), (0, 0)))
    )
    first_grad = edge_grads[:, :, 0]
    last_grad = edge_grads[:, :, 1]
    total = interior.at[:, :, 0, :].add(first_grad[:, :, 0:height])
    total = total.at[:, :, columns - 1, :].add(last_grad[:, :, 0:height])
    total = total.at[:, :, :, 0].add(first_grad[:, :, height:line_len])
    total = total.at[:, :, :, height - 1].add(last_grad[:, :, height:line_len])
    return total


def padded_input(field):
    return sphere_pad_local(whole_channels(field))


def convolve(padded, kernel):
    return lax.conv_general_dilated(
        padded,
        kernel,
        (1, 1),
        "VALID",
        dimension_numbers=("CNHW", "HWIO", "CNHW"),
        preferred_element_type=jnp.float32,
    )


def spread(cotangent, kernel):
    flipped = jnp.flip(kernel, (0, 1)).transpose(0, 1, 3, 2)
    return lax.conv_general_dilated(
        cotangent,
        flipped,
        (1, 1),
        ((2, 2), (2, 2)),
        dimension_numbers=("CNHW", "HWIO", "CNHW"),
        preferred_element_type=jnp.float32,
    )


def weight_terms(padded, cotangent):
    columns = cotangent.shape[2]
    height = cotangent.shape[3]
    flat_cot = cotangent.reshape(cotangent.shape[0], -1)
    tap_rows = []
    for col_tap in range(3):
        row_list = []
        for row_tap in range(3):
            tap_cells = padded[
                :, :, col_tap : col_tap + columns, row_tap : row_tap + height
            ].reshape(padded.shape[0], -1)
            row_list.append(
                lax.dot_general(
                    tap_cells,
                    flat_cot,
                    (((1,), (1,)), ((), ())),
                    preferred_element_type=jnp.float32,
                )
            )
        tap_rows.append(jnp.stack(row_list))
    return jnp.stack(tap_rows)


def on_device(fields, upstream, kernel_one, kernel_two):
    half_count = fields.shape[0]
    half_at = lax.axis_index("sub")
    face_side = fields.shape[2] * lax.axis_size("tile")
    cell_scale = 1.0 / (face_side * jnp.sqrt(jnp.float32(12.0)))
    out_one = lax.dynamic_slice_in_dim(kernel_one, half_at * half_count, half_count, 3)
    out_two = lax.dynamic_slice_in_dim(kernel_two, half_at * half_count, half_count, 3)
    in_one = lax.dynamic_slice_in_dim(kernel_one, half_at * half_count, half_count, 2)
    in_two = lax.dynamic_slice_in_dim(kernel_two, half_at * half_count, half_count, 2)
    padded_one = padded_input(fields)
    pre_one = convolve(padded_one, out_one)
    hidden = activate(pre_one).astype(jnp.bfloat16)
    padded_two = padded_input(hidden)
    result = convolve(padded_two, out_two).astype(jnp.bfloat16)
    hidden_grad = sphere_fold_local(spread(whole_channels(upstream), in_two))
    unused, pullback = jax.vjp(activate, pre_one)
    pre_grad = pullback(hidden_grad)[0].astype(jnp.bfloat16)
    fields_grad = sphere_fold_local(spread(whole_channels(pre_grad), in_one)).astype(jnp.bfloat16)
    kernel_one_grad = weight_terms(padded_one, pre_grad) * cell_scale
    kernel_two_grad = weight_terms(padded_two, upstream) * cell_scale
    kernel_one_grad, kernel_two_grad = lax.psum(
        (kernel_one_grad, kernel_two_grad), ("tile", "face")
    )
    return (result, fields_grad, kernel_one_grad, kernel_two_grad)


def solution(mesh):
    placed = (P("sub", "face", "tile", "parts"), P("sub", "face", "tile", "parts"), P(), P())
    return jax.shard_map(
        on_device,
        mesh=mesh,
        in_specs=placed,
        out_specs=(
            P("sub", "face", "tile", "parts"),
            P("sub", "face", "tile", "parts"),
            P("parts", None, None, "sub"),
            P("parts", None, None, "sub"),
        ),
        check_vma=False,
    )
```

profile of v0, /device:TPU:0, one launch (start us, length us, event | category | flops | bytes accessed | tf_op | source)
XLA Modules:
  0.0 541.0 jit_solution(8414374650207984221)
XLA Ops:
  12.9 5.0 collective-permute-start.1
  23.0 19.7 %all_gather.18 = f32[96,2,2,64]{0,2,1,3:T(2,128)S(1)} all-gather(f32[96,2,2,4]{0,2,1,3:T(2,128)S(1)} %copy.966), channel_id=1, replica_groups=mesh['parts'=1,'tile'=16,'face'=2,'sub'=1] {'tile'}, dimensions={3}, use_global_device_ids=true | all-gather | bytes 104448 | tf_op jit(solution)/shard_map/all_gather | solution.py:57
  46.4 5.7 %collective-permute-done.2 = f32[96,1,4,98]{3,0,1,2:T(8,128)S(1)} collective-permute-done((f32[96,1,4,98]{3,0,1,2:T(8,128)S(1)}, f32[96,1,4,98]{3,0,1,2:T(8,128)S(1)}, u32[]{:S(2)}, u32[]{:S(2)}) %collective-permute-start.2) | collective-permute-done | bytes 150560 | tf_op jit(solution)/shard_map/ppermute | solution.py:24
  55.9 62.0 %all-reduce.18 = (bf16[96,2,32]{2,0,1:T(8,128)(2,1)S(1)}, bf16[96,2,32]{2,0,1:T(8,128)(2,1)S(1)}, f32[96,2,32]{2,0,1:T(8,128)}, f32[96,2,32]{2,0,1:T(8,128)}) all-reduce(f32[96,2,32]{2,0,1:T(8,128)S(1)} %get-tuple-element.373, f32[96,2,32]{2,0,1:T(8,128)S(1)} %get-tuple-element.372, ...), channel_id=1, replica_groups=mesh['parts'=1,'tile'=16,'face'=2,'sub'=1] {'tile'}, use_global_device_ids=true, to_apply=%region_1.2 | all-reduce | flops 24576 | bytes 172032 | tf_op jit(solution)/shard_map/psum | solution.py:33
  122.8 17.5 %all_gather.16 = f32[96,2,2,64]{0,2,1,3:T(2,128)S(1)} all-gather(f32[96,2,2,4]{0,2,1,3:T(2,128)S(1)} %pad.117.clone), channel_id=1, replica_groups=mesh['parts'=1,'tile'=16,'face'=2,'sub'=1] {'tile'}, dimensions={3}, use_global_device_ids=true | all-gather | bytes 104448 | tf_op jit(solution)/shard_map/all_gather | solution.py:57
  149.5 15.8 %collective-permute-start.5 = (f32[96,2,1,98]{3,0,1,2:T(8,128)}, f32[96,2,1,98]{3,0,1,2:T(8,128)S(1)}, u32[]{:S(2)}, u32[]{:S(2)}) collective-permute-start(f32[96,2,1,98]{3,0,1,2:T(8,128)} %get-tuple-element.389), channel_id=1, source_target_pairs={{2,0},{4,2},{6,4},{8,6},{10,8},{12,10},{14,12},{16,14},{18,16},{20... | collective-permute-start | bytes 225800 | tf_op jit(solution)/shard_map/ppermute | solution.py:24
  170.1 4.4 collective-permute-start.9
  180.8 6.0 %copy.1069 = f32[2,2,96,96]{0,3,1,2:T(8,128)} copy(f32[2,2,96,96]{3,0,2,1:T(2,128)} %slice.1337) | data formatting | bytes 294912
  188.5 5.9 %copy.1070 = f32[2,2,96,96]{0,3,1,2:T(8,128)} copy(f32[2,2,96,96]{3,0,2,1:T(2,128)} %slice.1338) | data formatting | bytes 294912
  196.2 5.9 %copy.1071 = f32[2,2,96,96]{0,3,1,2:T(8,128)} copy(f32[2,2,96,96]{3,0,2,1:T(2,128)} %slice.1339) | data formatting | bytes 294912
  203.9 6.0 %copy.1072 = f32[2,2,96,96]{0,3,1,2:T(8,128)} copy(f32[2,2,96,96]{3,0,2,1:T(2,128)} %slice.1340) | data formatting | bytes 294912
  214.6 17.5 %all_gather.17 = f32[96,2,2,64]{0,2,1,3:T(2,128)S(1)} all-gather(f32[96,2,2,4]{0,2,1,3:T(2,128)S(1)} %pad.120.clone), channel_id=1, replica_groups=mesh['parts'=1,'tile'=16,'face'=2,'sub'=1] {'tile'}, dimensions={3}, use_global_device_ids=true | all-gather | bytes 104448 | tf_op jit(solution)/shard_map/all_gather | solution.py:57
  237.7 5.7 %copy.974 = f32[96,2,2,96]{2,0,1,3:T(8,128)} copy(f32[96,2,2,96]{3,0,1,2:T(8,128)S(1)} %fusion.95) | data formatting | bytes 294912 | tf_op jit(solution)/shard_map/scatter-add | solution.py:186
  247.0 16.7 %fusion.2 = bf16[96,2,2,96]{2,0,1,3:T(8,128)(2,1)S(1)} fusion(f32[2,2,96,96]{0,3,1,2:T(8,128)} %copy.1072, f32[96,2,2,96]{2,0,1,3:T(8,128)} %fusion.91, f32[2,2,96,96]{0,3,1,2:T(8,128)} %copy.1069, f32[2,2,96,96]{0,3,1,2:T(8,128)} %copy.1071, f32[2,2,96,96]{0,3,1,2:T(8,128)} %copy.1070), kind=kLoop, calls=%fused_computation.4 | loop fusion | flops 368640 | bytes 811008 | tf_op jit(solution)/shard_map/convert_element_type | solution.py:258
  271.5 5.2 copy.983
  278.1 63.9 %all-reduce.19 = (bf16[96,2,32]{2,0,1:T(8,128)(2,1)S(1)}, bf16[96,2,32]{2,0,1:T(8,128)(2,1)S(1)}, f32[96,2,32]{2,0,1:T(8,128)}, f32[96,2,32]{2,0,1:T(8,128)S(1)}) all-reduce(f32[96,2,32]{2,0,1:T(8,128)S(1)} %copy-done.8, f32[96,2,32]{2,0,1:T(8,128)S(1)} %copy-done.7, ...), channel_id=1, replica_groups=mesh['parts'=1,'tile'=16,'face'=2,'sub'=1] {'tile'}, use_global_device_ids=true, to_apply=%region_3.4 | all-reduce | flops 24576 | bytes 172032 | tf_op jit(solution)/shard_map/psum | solution.py:33
  350.2 5.5 %copy.995 = bf16[96,2,2,96]{3,0,2,1:T(8,128)(2,1)S(1)} copy(bf16[96,2,2,96]{2,0,1,3:T(8,128)(2,1)} %copy-done.1) | data formatting | bytes 147456 | tf_op jit(solution)/shard_map/convert_element_type | solution.py:258
  363.1 17.7 %all_gather.19 = f32[96,2,2,64]{0,2,1,3:T(2,128)S(1)} all-gather(f32[96,2,2,4]{0,2,1,3:T(2,128)S(1)} %copy.988), channel_id=1, replica_groups=mesh['parts'=1,'tile'=16,'face'=2,'sub'=1] {'tile'}, dimensions={3}, use_global_device_ids=true | all-gather | bytes 104448 | tf_op jit(solution)/shard_map/all_gather | solution.py:57
  386.6 4.1 collective-permute-start.13
  402.7 6.6 %collective-permute-done.14 = f32[96,1,6,98]{3,0,1,2:T(8,128)S(1)} collective-permute-done((f32[96,1,6,98]{3,0,1,2:T(8,128)S(1)}, f32[96,1,6,98]{3,0,1,2:T(8,128)S(1)}, u32[]{:S(2)}, u32[]{:S(2)}) %collective-permute-start.14) | collective-permute-done | bytes 225824 | tf_op jit(solution)/shard_map/ppermute | solution.py:22
  413.5 5.7 %copy.993 = f32[96,2,2,96]{2,0,1,3:T(8,128)} copy(f32[96,2,2,96]{3,0,1,2:T(8,128)S(1)} %fusion.81) | data formatting | bytes 294912 | tf_op jit(solution)/shard_map/scatter-add | solution.py:186
  422.9 7.1 %convert_element_type.73 = bf16[96,2,2,96]{2,0,1,3:T(8,128)(2,1)} convert(f32[96,2,2,96]{2,0,1,3:T(8,128)} %fusion.77) | non-fusion elementwise | flops 36864 | bytes 221184 | tf_op jit(solution)/shard_map/convert_element_type | solution.py:259
  430.0 6.2 %copy.1028 = bf16[96,2,2,96]{3,2,1,0:T(2,128)(2,1)} copy(bf16[96,2,2,96]{2,0,1,3:T(8,128)(2,1)} %convert_element_type.73) | data formatting | bytes 147456
  436.2 94.0 %all-reduce.17.cloned.1.call-done = (f32[3,3,96,96]{3,2,1,0:T(8,128)}, f32[3,3,96,96]{3,2,1,0:T(8,128)}) async-done(((f32[3,3,96,96]{3,2,1,0:T(8,128)}, f32[3,3,96,96]{3,2,1,0:T(8,128)}), (f32[3,3,96,96]{3,2,1,0:T(8,128)}, f32[3,3,96,96]{3,2,1,0:T(8,128)})) %all-reduce.17.cloned.1.call-update) | async-done | bytes 663568 | tf_op jit(solution)/shard_map/psum | solution.py:262
  (263 shorter events, 115.5 us)
Async XLA Ops:
  7.2 134.7 %copy-start = (bf16[3,3,96,96]{3,2,1,0:T(8,128)(2,1)S(1)}, bf16[3,3,96,96]{3,2,1,0:T(8,128)(2,1)}, u32[]{:S(2)}) copy-start(bf16[3,3,96,96]{3,2,1,0:T(8,128)(2,1)} %param.54) | copy-start | bytes 497668
  7.2 523.0 %all-reduce.17.cloned.1.call-start = ((), (), s32[]{:S(2)}) async-start(), calls=%async_computation | async-start | bytes 1769472 | tf_op jit(solution)/shard_map/psum | solution.py:262
  12.3 31.9 %collective-permute-start = (f32[96,2,1,98]{3,0,1,2:T(8,128)S(1)}, f32[96,2,1,98]{3,0,1,2:T(8,128)S(1)}, u32[]{:S(2)}, u32[]{:S(2)}) collective-permute-start(f32[96,2,1,98]{3,0,1,2:T(8,128)S(1)} %get-tuple-element.390), channel_id=1, source_target_pairs={{0,2},{2,4},{4,6},{6,8},{8,10},{10,12},{12,14},{14,16},{16,18},{18... | collective-permute-start | bytes 225800 | tf_op jit(solution)/shard_map/ppermute | solution.py:22
  12.9 31.4 %collective-permute-start.1 = (f32[96,2,1,98]{3,0,1,2:T(8,128)S(1)}, f32[96,2,1,98]{3,0,1,2:T(8,128)S(1)}, u32[]{:S(2)}, u32[]{:S(2)}) collective-permute-start(f32[96,2,1,98]{3,0,1,2:T(8,128)S(1)} %get-tuple-element.391), channel_id=1, source_target_pairs={{2,0},{4,2},{6,4},{8,6},{10,8},{12,10},{14,12},{16,14},{18,16},{20... | collective-permute-start | bytes 225800 | tf_op jit(solution)/shard_map/ppermute | solution.py:24
  19.0 122.8 %copy-start.18 = (pred[16,13]{0,1:T(8,128)(4,1)S(1)}, pred[16,13]{0,1:T(8,128)(4,1)}, u32[]{:S(2)}) copy-start(pred[16,13]{0,1:T(8,128)(4,1)} %constant.743) | copy-start | bytes 628
  44.3 7.8 %collective-permute-start.2 = (f32[96,1,4,98]{3,0,1,2:T(8,128)S(1)}, f32[96,1,4,98]{3,0,1,2:T(8,128)S(1)}, u32[]{:S(2)}, u32[]{:S(2)}) collective-permute-start(f32[96,1,4,98]{3,0,1,2:T(8,128)S(1)} %get-tuple-element.374), channel_id=1, source_target_pairs={{1,0},{0,1},{3,2},{2,3},{5,4},{4,5},{7,6},{6,7},{9,8},{8,9},{11,10... | collective-permute-start | bytes 451592 | tf_op jit(solution)/shard_map/ppermute | solution.py:24
  45.9 9.9 %collective-permute-start.3 = (f32[96,1,4,98]{3,0,1,2:T(8,128)S(1)}, f32[96,1,4,98]{3,0,1,2:T(8,128)S(1)}, u32[]{:S(2)}, u32[]{:S(2)}) collective-permute-start(f32[96,1,4,98]{3,0,1,2:T(8,128)S(1)} %get-tuple-element.375), channel_id=1, source_target_pairs={{0,1},{1,0},{2,3},{3,2},{4,5},{5,4},{6,7},{7,6},{8,9},{9,8},{10,11... | collective-permute-start | bytes 451592 | tf_op jit(solution)/shard_map/ppermute | solution.py:22
  121.7 56.6 %copy-start.2 = (bf16[96,2,2,96]{3,2,1,0:T(2,128)(2,1)S(1)}, bf16[96,2,2,96]{3,2,1,0:T(2,128)(2,1)}, u32[]{:S(2)}) copy-start(bf16[96,2,2,96]{3,2,1,0:T(2,128)(2,1)} %param.53) | copy-start | bytes 221188
  149.2 26.2 %collective-permute-start.4 = (f32[96,2,1,98]{3,0,1,2:T(8,128)}, f32[96,2,1,98]{3,0,1,2:T(8,128)S(1)}, u32[]{:S(2)}, u32[]{:S(2)}) collective-permute-start(f32[96,2,1,98]{3,0,1,2:T(8,128)} %get-tuple-element.388), channel_id=1, source_target_pairs={{0,2},{2,4},{4,6},{6,8},{8,10},{10,12},{12,14},{14,16},{16,18},{18... | collective-permute-start | bytes 225800 | tf_op jit(solution)/shard_map/ppermute | solution.py:22
  149.5 25.9 %collective-permute-start.5 = (f32[96,2,1,98]{3,0,1,2:T(8,128)}, f32[96,2,1,98]{3,0,1,2:T(8,128)S(1)}, u32[]{:S(2)}, u32[]{:S(2)}) collective-permute-start(f32[96,2,1,98]{3,0,1,2:T(8,128)} %get-tuple-element.389), channel_id=1, source_target_pairs={{2,0},{4,2},{6,4},{8,6},{10,8},{12,10},{14,12},{16,14},{18,16},{20... | collective-permute-start | bytes 225800 | tf_op jit(solution)/shard_map/ppermute | solution.py:24
  170.1 39.7 %collective-permute-start.8 = (f32[96,4,1,98]{3,0,1,2:T(8,128)}, f32[96,4,1,98]{3,0,1,2:T(8,128)S(1)}, u32[]{:S(2)}, u32[]{:S(2)}) collective-permute-start(f32[96,4,1,98]{3,0,1,2:T(8,128)} %get-tuple-element.350), channel_id=1, source_target_pairs={{0,2},{2,4},{4,6},{6,8},{8,10},{10,12},{12,14},{14,16},{16,18},{18... | collective-permute-start | bytes 451592 | tf_op jit(solution)/shard_map/ppermute | solution.py:22
  170.1 39.7 %collective-permute-start.9 = (f32[96,4,1,98]{3,0,1,2:T(8,128)}, f32[96,4,1,98]{3,0,1,2:T(8,128)S(1)}, u32[]{:S(2)}, u32[]{:S(2)}) collective-permute-start(f32[96,4,1,98]{3,0,1,2:T(8,128)} %get-tuple-element.351), channel_id=1, source_target_pairs={{2,0},{4,2},{6,4},{8,6},{10,8},{12,10},{14,12},{16,14},{18,16},{20... | collective-permute-start | bytes 451592 | tf_op jit(solution)/shard_map/ppermute | solution.py:24
  176.2 36.5 %collective-permute-start.6 = (f32[96,1,4,98]{3,0,1,2:T(8,128)}, f32[96,1,4,98]{3,0,1,2:T(8,128)S(1)}, u32[]{:S(2)}, u32[]{:S(2)}) collective-permute-start(f32[96,1,4,98]{3,0,1,2:T(8,128)} %get-tuple-element.368), channel_id=1, source_target_pairs={{1,0},{0,1},{3,2},{2,3},{5,4},{4,5},{7,6},{6,7},{9,8},{8,9},{11,10... | collective-permute-start | bytes 451592 | tf_op jit(solution)/shard_map/ppermute | solution.py:24
  177.7 35.0 %collective-permute-start.7 = (f32[96,1,4,98]{3,0,1,2:T(8,128)}, f32[96,1,4,98]{3,0,1,2:T(8,128)S(1)}, u32[]{:S(2)}, u32[]{:S(2)}) collective-permute-start(f32[96,1,4,98]{3,0,1,2:T(8,128)} %get-tuple-element.369), channel_id=1, source_target_pairs={{0,1},{1,0},{2,3},{3,2},{4,5},{5,4},{6,7},{7,6},{8,9},{9,8},{10,11... | collective-permute-start | bytes 451592 | tf_op jit(solution)/shard_map/ppermute | solution.py:22
  210.7 24.3 %collective-permute-start.10 = (f32[96,1,6,98]{3,0,1,2:T(8,128)}, f32[96,1,6,98]{3,0,1,2:T(8,128)}, u32[]{:S(2)}, u32[]{:S(2)}) collective-permute-start(f32[96,1,6,98]{3,0,1,2:T(8,128)} %get-tuple-element.346), channel_id=1, source_target_pairs={{0,1},{1,0},{2,3},{3,2},{4,5},{5,4},{6,7},{7,6},{8,9},{9,8},{10,11... | collective-permute-start | bytes 677384 | tf_op jit(solution)/shard_map/ppermute | solution.py:22
  212.2 22.8 %collective-permute-start.11 = (f32[96,1,6,98]{3,0,1,2:T(8,128)}, f32[96,1,6,98]{3,0,1,2:T(8,128)}, u32[]{:S(2)}, u32[]{:S(2)}) collective-permute-start(f32[96,1,6,98]{3,0,1,2:T(8,128)} %get-tuple-element.347), channel_id=1, source_target_pairs={{1,0},{0,1},{3,2},{2,3},{5,4},{4,5},{7,6},{6,7},{9,8},{8,9},{11,10... | collective-permute-start | bytes 677384 | tf_op jit(solution)/shard_map/ppermute | solution.py:24
  267.4 77.7 %copy-start.6 = (bf16[96,2,1,96]{3,0,2,1:T(8,128)(2,1)S(1)}, bf16[96,2,1,96]{3,0,2,1:T(8,128)(2,1)}, u32[]{:S(2)}) copy-start(bf16[96,2,1,96]{3,0,2,1:T(8,128)(2,1)} %copy-done.5) | copy-start | bytes 110596
  271.5 84.4 %copy-start.4 = (bf16[96,2,4,97]{3,0,2,1:T(8,128)(2,1)S(1)}, bf16[96,2,4,97]{3,0,2,1:T(8,128)(2,1)}, u32[]{:S(2)}) copy-start(bf16[96,2,4,97]{3,0,2,1:T(8,128)(2,1)} %get-tuple-element.383) | copy-start | bytes 446980
  349.4 43.5 %copy-start.12 = (f32[1,96,96]{2,1,0:T(8,128)S(1)}, f32[1,96,96]{2,1,0:T(8,128)}, u32[]{:S(2)}) copy-start(f32[1,96,96]{2,1,0:T(8,128)} %convolution_bitcast_fusion.9) | copy-start | bytes 110596
  355.8 38.8 %copy-start.10 = (f32[1,96,96]{2,1,0:T(8,128)S(1)}, f32[1,96,96]{2,1,0:T(8,128)}, u32[]{:S(2)}) copy-start(f32[1,96,96]{2,1,0:T(8,128)} %convolution_bitcast_fusion.5) | copy-start | bytes 110596
  386.2 12.7 %collective-permute-start.12 = (f32[96,4,1,98]{3,0,1,2:T(8,128)S(1)}, f32[96,4,1,98]{3,0,1,2:T(8,128)S(1)}, u32[]{:S(2)}, u32[]{:S(2)}) collective-permute-start(f32[96,4,1,98]{3,0,1,2:T(8,128)S(1)} %get-tuple-element.348), channel_id=1, source_target_pairs={{0,2},{2,4},{4,6},{6,8},{8,10},{10,12},{12,14},{14,16},{16,18},{18... | collective-permute-start | bytes 451592 | tf_op jit(solution)/shard_map/ppermute | solution.py:22
  386.6 12.3 %collective-permute-start.13 = (f32[96,4,1,98]{3,0,1,2:T(8,128)S(1)}, f32[96,4,1,98]{3,0,1,2:T(8,128)S(1)}, u32[]{:S(2)}, u32[]{:S(2)}) collective-permute-start(f32[96,4,1,98]{3,0,1,2:T(8,128)S(1)} %get-tuple-element.349), channel_id=1, source_target_pairs={{2,0},{4,2},{6,4},{8,6},{10,8},{12,10},{14,12},{16,14},{18,16},{20... | collective-permute-start | bytes 451592 | tf_op jit(solution)/shard_map/ppermute | solution.py:24
  398.9 10.4 %collective-permute-start.14 = (f32[96,1,6,98]{3,0,1,2:T(8,128)S(1)}, f32[96,1,6,98]{3,0,1,2:T(8,128)S(1)}, u32[]{:S(2)}, u32[]{:S(2)}) collective-permute-start(f32[96,1,6,98]{3,0,1,2:T(8,128)S(1)} %get-tuple-element.344), channel_id=1, source_target_pairs={{0,1},{1,0},{2,3},{3,2},{4,5},{5,4},{6,7},{7,6},{8,9},{9,8},{10,11... | collective-permute-start | bytes 677384 | tf_op jit(solution)/shard_map/ppermute | solution.py:22
  400.5 12.6 %collective-permute-start.15 = (f32[96,1,6,98]{3,0,1,2:T(8,128)S(1)}, f32[96,1,6,98]{3,0,1,2:T(8,128)S(1)}, u32[]{:S(2)}, u32[]{:S(2)}) collective-permute-start(f32[96,1,6,98]{3,0,1,2:T(8,128)S(1)} %get-tuple-element.345), channel_id=1, source_target_pairs={{1,0},{0,1},{3,2},{2,3},{5,4},{4,5},{7,6},{6,7},{9,8},{8,9},{11,10... | collective-permute-start | bytes 677384 | tf_op jit(solution)/shard_map/ppermute | solution.py:24
  (12 other events, 270.4 us)
Sparse Core Ops, SparseCore 0:
  402.8 127.3 all-reduce.16
where the time goes:
time: 551 us; the launch traced here: 541 us
  blocking collectives  198 us (36%)
  waiting for transfers between devices  114 us (21%)
  local copies, waits for them, and re-layouts  103 us (19%)
  other arithmetic  50.8 us (9%)
  starting transfers between devices  39 us (7%)
  matrix products  20.9 us (4%)
  between operations  15.6 us (3%)
    psum x2, blocking collectives, spread_2(): return lax.psum(block, axis)  126 us
    psum x1, waiting for transfers between devices, on_device(): lax.psum((kernel_one_grad, kernel_two_grad), ('tile', 'face'))  94 us
    all_gather x4, blocking collectives, collect_rows(): return lax.all_gather(pieces, 'tile', axis=3, tiled=True)  72.3 us
    unnamed x63, local copies, waits for them, and re-layouts  47 us
    ppermute x8, starting transfers between devices, extended(): lax.ppermute(head, axis, [((i + 1) % count, i) for i in range(count)])  33.5 us
    convert_element_type x1, other arithmetic, on_device(): pre_grad = pullback(hidden_grad)[0].astype(jnp.bfloat16)  16.7 us
    dot_general x18, matrix products, weight_terms(): lax.dot_general(tap_cells, flat_cot, (((1,), (1,)), ((), ())), preferred_...  13.9 us
    scatter-add x2, local copies, waits for them, and re-layouts, sphere_fold_local(): total = total.at[:, :, columns - 1, :].add(last_grad[:, :, 0:height])  11.4 us
  transfers between devices with their start and end apart: 17, of which 5 were waited for; matrix products, arithmetic and copies ran while one was open for 15% of the time, Pallas kernels for 0%

commit v1 on v0

--- a/solution.py
+++ b/solution.py
@@ -30,7 +30,7 @@
 
 def spread_2(block, axis, source):
     block = jnp.where(lax.axis_index(axis) == source, block, jnp.zeros_like(block))
-    return lax.psum(block, axis)
+    return jnp.sum(lax.all_gather(block, axis), axis=0)
 
 
 def activate(values):

time: 551 us -> 628 us (1.14)
  blocking collectives: 198 us -> 287 us
  starting transfers between devices: 39 us -> 17.8 us
  other arithmetic: 50.8 us -> 67.2 us
    all_gather x0 -> x8, blocking collectives: none -> 214 us  [spread_2(): return jnp.sum(lax.all_gather(block, axis), axis=0)]
    psum x2 -> x0, blocking collectives: 126 us -> none  [spread_2(): return lax.psum(block, axis)]
    ppermute x8, starting transfers between devices: 33.5 us -> 15.6 us  [extended(): lax.ppermute(head, axis, [((i + 1) % count, i) for i in range(count)])]
    reduce_sum x0 -> x8, other arithmetic: none -> 9.53 us  [spread_2(): return jnp.sum(lax.all_gather(block, axis), axis=0)]
    unnamed x63 -> x79, local copies, waits for them, and re-layouts: 47 us -> 41.7 us
  transfers between devices with their start and end apart: 17 -> 17, of which waited for: 5 -> 6; matrix products, arithmetic and copies ran while one was open for 15% -> 29% of each run, Pallas kernels for 0% -> 0%
where the time goes in v1:
time: 628 us; the launch traced here: 618 us
  blocking collectives  287 us (46%)
  waiting for transfers between devices  108 us (17%)
  local copies, waits for them, and re-layouts  106 us (17%)
  other arithmetic  67.2 us (11%)
  starting transfers between devices  17.8 us (3%)
  matrix products  16.4 us (3%)
  between operations  15.8 us (3%)
    all_gather x8, blocking collectives, spread_2(): return jnp.sum(lax.all_gather(block, axis), axis=0)  214 us
    psum x1, waiting for transfers between devices, on_device(): lax.psum((kernel_one_grad, kernel_two_grad), ('tile', 'face'))  88 us
    all_gather x4, blocking collectives, collect_rows(): return lax.all_gather(pieces, 'tile', axis=3, tiled=True)  72.6 us
    unnamed x79, local copies, waits for them, and re-layouts  41.7 us
    convert_element_type x1, other arithmetic, on_device(): pre_grad = pullback(hidden_grad)[0].astype(jnp.bfloat16)  16.7 us
    ppermute x8, starting transfers between devices, extended(): lax.ppermute(head, axis, [((i + 1) % count, i) for i in range(count)])  15.6 us
  transfers between devices with their start and end apart: 17, of which 6 were waited for; matrix products, arithmetic and copies ran while one was open for 29% of the time, Pallas kernels for 0%

profile of v1, /device:TPU:0, one launch (start us, length us, event | category | flops | bytes accessed | tf_op | source)
XLA Modules:
  0.0 618.4 jit_solution(12377827224274308233)
XLA Ops:
  13.0 5.5 collective-permute-start.1
  25.6 24.8 %all-gather.5 = f32[1536,2,32]{2,1,0:T(2,128)S(1)} all-gather(f32[96,2,32]{2,1,0:T(2,128)S(1)} %copy.1068), channel_id=7, replica_groups=mesh['parts'=1,'tile'=16,'face'=2,'sub'=1] {'tile'}, dimensions={0}, use_global_device_ids=true | all-gather | bytes 417792 | tf_op jit(solution)/shard_map/all_gather | solution.py:33
  52.8 26.4 %all-gather.4 = f32[1536,2,32]{2,1,0:T(2,128)S(1)} all-gather(f32[96,2,32]{2,1,0:T(2,128)S(1)} %copy.1066), channel_id=6, replica_groups=mesh['parts'=1,'tile'=16,'face'=2,'sub'=1] {'tile'}, dimensions={0}, use_global_device_ids=true | all-gather | bytes 417792 | tf_op jit(solution)/shard_map/all_gather | solution.py:33
  86.0 17.8 %all_gather.66 = f32[96,2,2,64]{0,2,1,3:T(2,128)S(1)} all-gather(f32[96,2,2,4]{0,2,1,3:T(2,128)S(1)} %copy.1072), channel_id=1, replica_groups=mesh['parts'=1,'tile'=16,'face'=2,'sub'=1] {'tile'}, dimensions={3}, use_global_device_ids=true | all-gather | bytes 104448 | tf_op jit(solution)/shard_map/all_gather | solution.py:57
  120.2 38.7 %all-gather.1 = f32[1536,2,1,32]{3,1,2,0:T(2,128)S(1)} all-gather(f32[96,2,1,32]{3,1,2,0:T(2,128)S(1)} %copy.1036), channel_id=3, replica_groups=mesh['parts'=1,'tile'=16,'face'=2,'sub'=1] {'tile'}, dimensions={0}, use_global_device_ids=true | all-gather | bytes 417792 | tf_op jit(solution)/shard_map/all_gather | solution.py:33
  160.9 24.8 %all-gather = f32[1536,2,1,32]{3,1,2,0:T(2,128)S(1)} all-gather(f32[96,2,1,32]{3,1,2,0:T(2,128)S(1)} %copy.1027), channel_id=2, replica_groups=mesh['parts'=1,'tile'=16,'face'=2,'sub'=1] {'tile'}, dimensions={0}, use_global_device_ids=true | all-gather | bytes 417792 | tf_op jit(solution)/shard_map/all_gather | solution.py:33
  188.0 18.3 %all_gather.57 = f32[96,2,2,64]{0,2,1,3:T(2,128)S(1)} all-gather(f32[96,2,2,4]{0,2,1,3:T(2,128)S(1)} %pad.117.clone), channel_id=1, replica_groups=mesh['parts'=1,'tile'=16,'face'=2,'sub'=1] {'tile'}, dimensions={3}, use_global_device_ids=true | all-gather | bytes 104448 | tf_op jit(solution)/shard_map/all_gather | solution.py:57
  235.9 5.2 copy.1180
  247.4 5.5 copy.1080
  256.5 16.7 %fusion.2 = bf16[96,2,2,96]{2,0,1,3:T(8,128)(2,1)S(1)} fusion(f32[2,2,96,96]{0,3,1,2:T(8,128)} %copy.1182, f32[96,2,2,96]{2,0,1,3:T(8,128)} %fusion.91, f32[2,2,96,96]{0,3,1,2:T(8,128)} %copy.1179, f32[2,2,96,96]{0,3,1,2:T(8,128)} %copy.1181, f32[2,2,96,96]{0,3,1,2:T(8,128)} %copy.1180), kind=kLoop, calls=%fused_computation.4 | loop fusion | flops 368640 | bytes 811008 | tf_op jit(solution)/shard_map/convert_element_type | solution.py:258
  280.9 5.2 copy.1089
  289.1 5.5 copy.1105
  304.1 25.4 %all-gather.6 = f32[1536,2,32]{2,1,0:T(2,128)S(1)} all-gather(f32[96,2,32]{2,1,0:T(2,128)S(1)} %copy.1092), channel_id=8, replica_groups=mesh['parts'=1,'tile'=16,'face'=2,'sub'=1] {'tile'}, dimensions={0}, use_global_device_ids=true | all-gather | bytes 417792 | tf_op jit(solution)/shard_map/all_gather | solution.py:33
  333.9 23.5 %all-gather.7 = f32[1536,2,32]{2,1,0:T(2,128)S(1)} all-gather(f32[96,2,32]{2,1,0:T(2,128)S(1)} %copy.1094), channel_id=9, replica_groups=mesh['parts'=1,'tile'=16,'face'=2,'sub'=1] {'tile'}, dimensions={0}, use_global_device_ids=true | all-gather | bytes 417792 | tf_op jit(solution)/shard_map/all_gather | solution.py:33
  363.2 18.2 %all_gather.71 = f32[96,2,2,64]{0,2,1,3:T(2,128)S(1)} all-gather(f32[96,2,2,4]{0,2,1,3:T(2,128)S(1)} %copy.1098), channel_id=1, replica_groups=mesh['parts'=1,'tile'=16,'face'=2,'sub'=1] {'tile'}, dimensions={3}, use_global_device_ids=true | all-gather | bytes 104448 | tf_op jit(solution)/shard_map/all_gather | solution.py:57
  390.2 25.2 %all-gather.3 = f32[1536,2,1,32]{3,1,2,0:T(2,128)S(1)} all-gather(f32[96,2,1,32]{3,1,2,0:T(2,128)S(1)} %copy.1056), channel_id=5, replica_groups=mesh['parts'=1,'tile'=16,'face'=2,'sub'=1] {'tile'}, dimensions={0}, use_global_device_ids=true | all-gather | bytes 417792 | tf_op jit(solution)/shard_map/all_gather | solution.py:33
  419.7 18.3 %all_gather.60 = f32[96,2,2,64]{0,2,1,3:T(2,128)S(1)} all-gather(f32[96,2,2,4]{0,2,1,3:T(2,128)S(1)} %pad.120.clone), channel_id=1, replica_groups=mesh['parts'=1,'tile'=16,'face'=2,'sub'=1] {'tile'}, dimensions={3}, use_global_device_ids=true | all-gather | bytes 104448 | tf_op jit(solution)/shard_map/all_gather | solution.py:57
  440.2 25.5 %all-gather.2 = f32[1536,2,1,32]{3,1,2,0:T(2,128)S(1)} all-gather(f32[96,2,1,32]{3,1,2,0:T(2,128)S(1)} %copy.1048), channel_id=4, replica_groups=mesh['parts'=1,'tile'=16,'face'=2,'sub'=1] {'tile'}, dimensions={0}, use_global_device_ids=true | all-gather | bytes 417792 | tf_op jit(solution)/shard_map/all_gather | solution.py:33
  480.1 7.6 %collective-permute-done.15 = f32[96,1,6,98]{3,0,1,2:T(8,128)S(1)} collective-permute-done((f32[96,1,6,98]{3,0,1,2:T(8,128)S(1)}, f32[96,1,6,98]{3,0,1,2:T(8,128)S(1)}, u32[]{:S(2)}, u32[]{:S(2)}) %collective-permute-start.15) | collective-permute-done | bytes 225824 | tf_op jit(solution)/shard_map/ppermute | solution.py:24
  487.8 6.5 %collective-permute-done.14 = f32[96,1,6,98]{3,0,1,2:T(8,128)S(1)} collective-permute-done((f32[96,1,6,98]{3,0,1,2:T(8,128)S(1)}, f32[96,1,6,98]{3,0,1,2:T(8,128)S(1)}, u32[]{:S(2)}, u32[]{:S(2)}) %collective-permute-start.14) | collective-permute-done | bytes 225824 | tf_op jit(solution)/shard_map/ppermute | solution.py:22
  497.0 5.6 copy.1103
  506.2 7.2 %convert_element_type.73 = bf16[96,2,2,96]{2,0,1,3:T(8,128)(2,1)} convert(f32[96,2,2,96]{2,0,1,3:T(8,128)} %fusion.77) | non-fusion elementwise | flops 36864 | bytes 221184 | tf_op jit(solution)/shard_map/convert_element_type | solution.py:259
  513.4 6.2 copy.1138
  519.5 88.0 %all-reduce.13.cloned.1.call-done = (f32[3,3,96,96]{3,2,1,0:T(8,128)}, f32[3,3,96,96]{3,2,1,0:T(8,128)}) async-done(((f32[3,3,96,96]{3,2,1,0:T(8,128)}, f32[3,3,96,96]{3,2,1,0:T(8,128)}), (f32[3,3,96,96]{3,2,1,0:T(8,128)}, f32[3,3,96,96]{3,2,1,0:T(8,128)})) %all-reduce.13.cloned.1.call-update) | async-done | bytes 663568 | tf_op jit(solution)/shard_map/psum | solution.py:262
  (306 shorter events, 151.3 us)
Async XLA Ops:
  7.2 201.9 %copy-start = (bf16[3,3,96,96]{3,2,1,0:T(8,128)(2,1)S(1)}, bf16[3,3,96,96]{3,2,1,0:T(8,128)(2,1)}, u32[]{:S(2)}) copy-start(bf16[3,3,96,96]{3,2,1,0:T(8,128)(2,1)} %param.54) | copy-start | bytes 497668
  7.2 600.4 %all-reduce.13.cloned.1.call-start = ((), (), s32[]{:S(2)}) async-start(), calls=%async_computation | async-start | bytes 1769472 | tf_op jit(solution)/shard_map/psum | solution.py:262
  13.0 94.3 %collective-permute-start.1 = (f32[96,2,1,98]{3,0,1,2:T(8,128)}, f32[96,2,1,98]{3,0,1,2:T(8,128)S(1)}, u32[]{:S(2)}, u32[]{:S(2)}) collective-permute-start(f32[96,2,1,98]{3,0,1,2:T(8,128)} %get-tuple-element.383), channel_id=1, source_target_pairs={{2,0},{4,2},{6,4},{8,6},{10,8},{12,10},{14,12},{16,14},{18,16},{20... | collective-permute-start | bytes 225800 | tf_op jit(solution)/shard_map/ppermute | solution.py:24
  18.4 88.8 %collective-permute-start = (f32[96,2,1,98]{3,0,1,2:T(8,128)}, f32[96,2,1,98]{3,0,1,2:T(8,128)S(1)}, u32[]{:S(2)}, u32[]{:S(2)}) collective-permute-start(f32[96,2,1,98]{3,0,1,2:T(8,128)} %get-tuple-element.382), channel_id=1, source_target_pairs={{0,2},{2,4},{4,6},{6,8},{8,10},{10,12},{12,14},{14,16},{16,18},{18... | collective-permute-start | bytes 225800 | tf_op jit(solution)/shard_map/ppermute | solution.py:22
  50.4 59.1 %copy-start.3 = (bf16[96,2,2,96]{3,2,1,0:T(2,128)(2,1)S(1)}, bf16[96,2,2,96]{3,2,1,0:T(2,128)(2,1)}, u32[]{:S(2)}) copy-start(bf16[96,2,2,96]{3,2,1,0:T(2,128)(2,1)} %param.52) | copy-start | bytes 221188
  105.6 4.9 collective-permute-start.9
  107.3 7.8 %collective-permute-start.8 = (f32[96,4,1,98]{3,0,1,2:T(8,128)S(1)}, f32[96,4,1,98]{3,0,1,2:T(8,128)S(1)}, u32[]{:S(2)}, u32[]{:S(2)}) collective-permute-start(f32[96,4,1,98]{3,0,1,2:T(8,128)S(1)} %get-tuple-element.342), channel_id=1, source_target_pairs={{0,2},{2,4},{4,6},{6,8},{8,10},{10,12},{12,14},{14,16},{16,18},{18... | collective-permute-start | bytes 451592 | tf_op jit(solution)/shard_map/ppermute | solution.py:22
  107.4 10.6 %collective-permute-start.2 = (f32[96,1,4,98]{3,0,1,2:T(8,128)S(1)}, f32[96,1,4,98]{3,0,1,2:T(8,128)S(1)}, u32[]{:S(2)}, u32[]{:S(2)}) collective-permute-start(f32[96,1,4,98]{3,0,1,2:T(8,128)S(1)} %get-tuple-element.366), channel_id=1, source_target_pairs={{1,0},{0,1},{3,2},{2,3},{5,4},{4,5},{7,6},{6,7},{9,8},{8,9},{11,10... | collective-permute-start | bytes 451592 | tf_op jit(solution)/shard_map/ppermute | solution.py:24
  108.9 10.5 %collective-permute-start.3 = (f32[96,1,4,98]{3,0,1,2:T(8,128)S(1)}, f32[96,1,4,98]{3,0,1,2:T(8,128)S(1)}, u32[]{:S(2)}, u32[]{:S(2)}) collective-permute-start(f32[96,1,4,98]{3,0,1,2:T(8,128)S(1)} %get-tuple-element.367), channel_id=1, source_target_pairs={{0,1},{1,0},{2,3},{3,2},{4,5},{5,4},{6,7},{7,6},{8,9},{9,8},{10,11... | collective-permute-start | bytes 451592 | tf_op jit(solution)/shard_map/ppermute | solution.py:22
  115.9 128.8 %collective-permute-start.11 = (f32[96,1,6,98]{3,0,1,2:T(8,128)}, f32[96,1,6,98]{3,0,1,2:T(8,128)}, u32[]{:S(2)}, u32[]{:S(2)}) collective-permute-start(f32[96,1,6,98]{3,0,1,2:T(8,128)} %get-tuple-element.339), channel_id=1, source_target_pairs={{1,0},{0,1},{3,2},{2,3},{5,4},{4,5},{7,6},{6,7},{9,8},{8,9},{11,10... | collective-permute-start | bytes 677384 | tf_op jit(solution)/shard_map/ppermute | solution.py:24
  117.4 127.3 %collective-permute-start.10 = (f32[96,1,6,98]{3,0,1,2:T(8,128)}, f32[96,1,6,98]{3,0,1,2:T(8,128)}, u32[]{:S(2)}, u32[]{:S(2)}) collective-permute-start(f32[96,1,6,98]{3,0,1,2:T(8,128)} %get-tuple-element.338), channel_id=1, source_target_pairs={{0,1},{1,0},{2,3},{3,2},{4,5},{5,4},{6,7},{7,6},{8,9},{9,8},{10,11... | collective-permute-start | bytes 677384 | tf_op jit(solution)/shard_map/ppermute | solution.py:22
  214.8 26.2 %copy-start.17 = (bf16[2,2,96,96]{2,3,0,1:T(8,128)(2,1)}, bf16[2,2,96,96]{2,3,0,1:T(8,128)(2,1)S(1)}, u32[]{:S(2)}) copy-start(bf16[2,2,96,96]{2,3,0,1:T(8,128)(2,1)S(1)} %copy.1190) | copy-start | bytes 221188
  217.9 23.9 %collective-permute-start.5 = (f32[96,2,1,98]{3,0,1,2:T(8,128)}, f32[96,2,1,98]{3,0,1,2:T(8,128)S(1)}, u32[]{:S(2)}, u32[]{:S(2)}) collective-permute-start(f32[96,2,1,98]{3,0,1,2:T(8,128)} %get-tuple-element.381), channel_id=1, source_target_pairs={{2,0},{4,2},{6,4},{8,6},{10,8},{12,10},{14,12},{16,14},{18,16},{20... | collective-permute-start | bytes 225800 | tf_op jit(solution)/shard_map/ppermute | solution.py:24
  219.1 22.7 %collective-permute-start.4 = (f32[96,2,1,98]{3,0,1,2:T(8,128)}, f32[96,2,1,98]{3,0,1,2:T(8,128)S(1)}, u32[]{:S(2)}, u32[]{:S(2)}) collective-permute-start(f32[96,2,1,98]{3,0,1,2:T(8,128)} %get-tuple-element.380), channel_id=1, source_target_pairs={{0,2},{2,4},{4,6},{6,8},{8,10},{10,12},{12,14},{14,16},{16,18},{18... | collective-permute-start | bytes 225800 | tf_op jit(solution)/shard_map/ppermute | solution.py:22
  242.7 145.9 %collective-permute-start.6 = (f32[96,1,4,98]{3,0,1,2:T(8,128)}, f32[96,1,4,98]{3,0,1,2:T(8,128)}, u32[]{:S(2)}, u32[]{:S(2)}) collective-permute-start(f32[96,1,4,98]{3,0,1,2:T(8,128)} %get-tuple-element.360), channel_id=1, source_target_pairs={{1,0},{0,1},{3,2},{2,3},{5,4},{4,5},{7,6},{6,7},{9,8},{8,9},{11,10... | collective-permute-start | bytes 451592 | tf_op jit(solution)/shard_map/ppermute | solution.py:24
  244.2 144.4 %collective-permute-start.7 = (f32[96,1,4,98]{3,0,1,2:T(8,128)}, f32[96,1,4,98]{3,0,1,2:T(8,128)}, u32[]{:S(2)}, u32[]{:S(2)}) collective-permute-start(f32[96,1,4,98]{3,0,1,2:T(8,128)} %get-tuple-element.361), channel_id=1, source_target_pairs={{0,1},{1,0},{2,3},{3,2},{4,5},{5,4},{6,7},{7,6},{8,9},{9,8},{10,11... | collective-permute-start | bytes 451592 | tf_op jit(solution)/shard_map/ppermute | solution.py:22
  329.5 59.1 %copy-start.7 = (f32[96,2,1,98]{3,0,1,2:T(8,128)S(1)}, f32[96,2,1,98]{3,0,1,2:T(8,128)}, u32[]{:S(2)}) copy-start(f32[96,2,1,98]{3,0,1,2:T(8,128)} %copy-done.6) | copy-start | bytes 225796
  329.5 59.1 %copy-start.9 = (f32[96,2,1,98]{3,0,1,2:T(8,128)S(1)}, f32[96,2,1,98]{3,0,1,2:T(8,128)}, u32[]{:S(2)}) copy-start(f32[96,2,1,98]{3,0,1,2:T(8,128)} %copy-done.8) | copy-start | bytes 225796
  384.0 92.3 %collective-permute-start.13 = (f32[96,4,1,98]{3,0,1,2:T(8,128)}, f32[96,4,1,98]{3,0,1,2:T(8,128)}, u32[]{:S(2)}, u32[]{:S(2)}) collective-permute-start(f32[96,4,1,98]{3,0,1,2:T(8,128)} %get-tuple-element.341), channel_id=1, source_target_pairs={{2,0},{4,2},{6,4},{8,6},{10,8},{12,10},{14,12},{16,14},{18,16},{20... | collective-permute-start | bytes 451592 | tf_op jit(solution)/shard_map/ppermute | solution.py:24
  385.2 91.1 %collective-permute-start.12 = (f32[96,4,1,98]{3,0,1,2:T(8,128)}, f32[96,4,1,98]{3,0,1,2:T(8,128)}, u32[]{:S(2)}, u32[]{:S(2)}) collective-permute-start(f32[96,4,1,98]{3,0,1,2:T(8,128)} %get-tuple-element.340), channel_id=1, source_target_pairs={{0,2},{2,4},{4,6},{6,8},{8,10},{10,12},{12,14},{14,16},{16,18},{18... | collective-permute-start | bytes 451592 | tf_op jit(solution)/shard_map/ppermute | solution.py:22
  416.4 58.2 %copy-start.26 = (pred[16,13]{0,1:T(8,128)(4,1)S(1)}, pred[16,13]{0,1:T(8,128)(4,1)}, u32[]{:S(2)}) copy-start(pred[16,13]{0,1:T(8,128)(4,1)} %constant.743) | copy-start | bytes 628
  476.1 20.8 %copy-start.4 = (f32[96,2,2,96]{3,0,1,2:T(8,128)S(1)}, f32[96,2,2,96]{3,0,1,2:T(8,128)}, u32[]{:S(2)}) copy-start(f32[96,2,2,96]{3,0,1,2:T(8,128)} %slice.1343) | copy-start | bytes 442372
  477.2 10.6 %collective-permute-start.15 = (f32[96,1,6,98]{3,0,1,2:T(8,128)S(1)}, f32[96,1,6,98]{3,0,1,2:T(8,128)S(1)}, u32[]{:S(2)}, u32[]{:S(2)}) collective-permute-start(f32[96,1,6,98]{3,0,1,2:T(8,128)S(1)} %get-tuple-element.337), channel_id=1, source_target_pairs={{1,0},{0,1},{3,2},{2,3},{5,4},{4,5},{7,6},{6,7},{9,8},{8,9},{11,10... | collective-permute-start | bytes 677384 | tf_op jit(solution)/shard_map/ppermute | solution.py:24
  478.7 15.5 %collective-permute-start.14 = (f32[96,1,6,98]{3,0,1,2:T(8,128)S(1)}, f32[96,1,6,98]{3,0,1,2:T(8,128)S(1)}, u32[]{:S(2)}, u32[]{:S(2)}) collective-permute-start(f32[96,1,6,98]{3,0,1,2:T(8,128)S(1)} %get-tuple-element.336), channel_id=1, source_target_pairs={{0,1},{1,0},{2,3},{3,2},{4,5},{5,4},{6,7},{7,6},{8,9},{9,8},{10,11... | collective-permute-start | bytes 677384 | tf_op jit(solution)/shard_map/ppermute | solution.py:22
  (20 other events, 138.5 us)
Sparse Core Ops, SparseCore 0:
  480.3 127.2 all-reduce.12
